TPU v7x, 256 devices: a whole 4x4x8 slice. The times are simulated.
256 devices in a mesh: gx: 16 (over y_lo, z), gy: 16 (over y_hi, x, core).
Axes of the slice: x: 4, y: 4 (y_hi: 2, y_lo: 2; y = y_hi * 2 + y_lo), z: 8, core: 2. Of those that a mesh axis runs over, the one named last changes fastest.
Arguments:
- obs_values: bfloat16 [4096, 48, 128], P(('gx', 'gy')), may hold values from -1.5 to 1.5
- obs_weight: float32 [4096, 128], P(('gx', 'gy')), may hold values from 0.25 to 4
- obs_box: int32 [4096, 128], P(('gx', 'gy')), may hold values from 0 to 127
- obs_owner: int32 [4096], P(('gx', 'gy')), may hold values from 0 to 255
- block_count: int32 [256], P(('gx', 'gy')), may hold values from 1 to 16, as said below
- diff_x: float32 [48, 128, 2048], P(None, 'gx', 'gy'), may hold values from 0.02 to 0.24
- diff_y: float32 [48, 128, 2048], P(None, 'gx', 'gy'), may hold values from 0.02 to 0.24
- spread_std: float32 [48, 128, 2048], P(None, 'gx', 'gy'), may hold values from 0.3 to 3
- land_sea: int32 [128, 2048], P('gx', 'gy'), may hold values 0 or 1
- vert_corr: float32 [48, 48], replicated, may hold values from -0.12268693 to 1.122687, as said below
Outputs:
- increment: float32 [48, 128, 2048], P(None, 'gx', 'gy')
Inputs may be any that keep to these rules, and one draw needn't show every extreme that they name: `block_count`: some device holds exactly 16 filled blocks in every draw. vert_corr is the identity plus a matrix E whose entries have magnitude at most 0.85 / sqrt(48); it is the same for all columns.
All inputs are finite; a program needn't handle non-finite values. No bound on the sum of `land_sea` on one device may be relied on, other than what follows from the above.
Results may differ from a plain program's by a relative error of at most 0.0003.
Values sent between devices are 32-bit elements; how exact they have to be, the bound alone decides.
A program may use at most 64 MiB of HBM per device.

v0:
```python
import jax
import jax.numpy as jnp
from jax import lax
from jax.sharding import PartitionSpec as P

BOX_DEV = 128
PASSES = 4
HIGH = lax.Precision.HIGHEST


def extended(block, sides, width):
    for axis, dim in sides:
        count = lax.axis_size(axis)
        forward = [(i, i + 1) for i in range(count - 1)]
        forward.append((count - 1, 0))
        backward = [(target, source) for source, target in forward]
        low = lax.ppermute(
            lax.slice_in_dim(block, block.shape[dim] - width, None, axis=dim), axis, forward
        )
        high = lax.ppermute(lax.slice_in_dim(block, 0, width, axis=dim), axis, backward)
        block = jnp.concatenate([low, block, high], axis=dim)
    return block


def one_pass(field, east, north):
    centre = field[:, 1:-1, 1:-1]
    out = centre + east[:, 1:-1, 1:-1] * (field[:, 2:, 1:-1] - centre)
    out = out + east[:, :-2, 1:-1] * (field[:, :-2, 1:-1] - centre)
    out = out + north[:, 1:-1, 1:-1] * (field[:, 1:-1, 2:] - centre)
    out = out + north[:, 1:-1, :-2] * (field[:, 1:-1, :-2] - centre)
    return out


def face_terms(padded, levels):
    diff_east = padded[:levels]
    diff_north = padded[levels : 2 * levels]
    mask = padded[2 * levels]
    east = diff_east[:, :-1, :] * (mask[:-1, :] * mask[1:, :])[None]
    north = diff_north[:, :, :-1] * (mask[:, :-1] * mask[:, 1:])[None]
    east = jnp.pad(east, ((0, 0), (0, 1), (0, 0)))
    north = jnp.pad(north, ((0, 0), (0, 0), (0, 1)))
    return (east, north)


def passes_round(padded, east, north):
    padded = one_pass(padded, east, north)
    return padded


def local(
    obs_values,
    obs_weight,
    obs_box,
    obs_owner,
    block_count,
    diff_x,
    diff_y,
    spread_std,
    land_sea,
    vert_corr,
):
    levels = diff_x.shape[0]
    width_x = diff_x.shape[1]
    width_y = diff_x.shape[2]
    blocks = obs_values.shape[0]
    box_count = BOX_DEV
    filled = (jnp.arange(blocks, dtype=jnp.int32) < block_count[0]).astype(jnp.float32)
    weighted = obs_values.astype(jnp.float32) * (obs_weight * filled[:, None])[:, None, :]
    onehot = (obs_box[:, :, None] == jnp.arange(box_count, dtype=jnp.int32)[None, None, :]).astype(
        jnp.float32
    )
    contrib = jnp.einsum("blo,bok->blk", weighted, onehot, precision=HIGH)
    by_level = lax.all_to_all(contrib, "gy", split_axis=1, concat_axis=0, tiled=True)
    owners = lax.all_gather(obs_owner, "gy", axis=0, tiled=True)
    targets = jnp.arange(lax.axis_size(("gx", "gy")) * 1, dtype=jnp.int32)
    select = (owners[None, :] == targets[:, None]).astype(jnp.float32)
    partial = jnp.einsum("rb,blk->rlk", select, by_level, precision=HIGH)
    mine = lax.psum_scatter(partial, "gx", scatter_dimension=0, tiled=True)
    superob = lax.all_to_all(mine, "gy", split_axis=0, concat_axis=1, tiled=True)[0]
    vbox = jnp.dot(vert_corr, superob, precision=HIGH)
    spread = vbox.reshape(levels, 8, 16)
    spread = jnp.repeat(jnp.repeat(spread, width_x // 8, axis=1), width_y // 16, axis=2)
    mask = land_sea.astype(jnp.float32)
    forcing = spread * spread_std * mask[None]
    depth = 1
    rounds = PASSES // depth
    moved = lax.all_to_all(
        jnp.stack([diff_x, diff_y]), "gy", split_axis=1, concat_axis=3, tiled=True
    )
    mask_whole = lax.all_gather(mask, "gy", axis=1, tiled=True)
    field = lax.all_to_all(forcing, "gy", split_axis=0, concat_axis=2, tiled=True)
    group = field.shape[0]
    stacked = jnp.concatenate([moved[0], moved[1], mask_whole[None]], axis=0)
    stacked = extended(stacked, (("gx", 1),), depth)
    stacked = jnp.pad(stacked, ((0, 0), (0, 0), (depth, depth)))
    east, north = face_terms(stacked, group)
    for turn in range(rounds):
        padded = extended(field, (("gx", 1),), depth)
        padded = jnp.pad(padded, ((0, 0), (0, 0), (depth, depth)))
        field = passes_round(padded, east, north)
    field = lax.all_to_all(field, "gy", split_axis=2, concat_axis=0, tiled=True)
    mixed = jnp.dot(vert_corr, field.reshape(levels, -1), precision=HIGH).reshape(
        levels, width_x, width_y
    )
    return mixed * spread_std * mask[None]


def solution(mesh):
    in_specs = (
        P(("gx", "gy"), None, None),
        P(("gx", "gy"), None),
        P(("gx", "gy"), None),
        P(("gx", "gy")),
        P(("gx", "gy")),
        P(None, "gx", "gy"),
        P(None, "gx", "gy"),
        P(None, "gx", "gy"),
        P("gx", "gy"),
        P(),
    )
    out_specs = P(None, "gx", "gy")
    return jax.shard_map(local, mesh=mesh, in_specs=in_specs, out_specs=out_specs, check_vma=False)
```

profile of v0, /device:TPU:1, one launch (start us, length us, event | category | flops | bytes accessed | tf_op | source)
XLA Modules:
  0.0 235.9 jit_solution(9146900084684502872)
XLA Ops:
  6.5 1.8 pad_maximum_fusion
  8.3 8.4 %all-to-all-start.3 = ((f32[2,48,8,128]{3,2,0,1:T(8,128)}), f32[2,48,8,128]{3,2,0,1:T(8,128)S(1)}, u32[]{:S(2)}, u32[]{:S(2)}) async-start(f32[2,48,8,128]{3,2,0,1:T(8,128)} %pad_maximum_fusion), calls=%async_computation.4 | async-start | bytes 786432 | tf_op jit(solution)/shard_map/all_to_all | solution.py:87
  18.9 1.7 fusion
  21.5 1.3 dynamic-slice
  24.2 11.3 %all-reduce.5 = s32[256]{0:T(256)S(1)} all-reduce(s32[256]{0:T(256)S(1)} %dynamic-update-slice), channel_id=1, replica_groups=mesh['gx'=16,'gy'=16] {'gy'}, use_global_device_ids=true, to_apply=%add.5 | all-reduce | flops 256 | bytes 2048
  35.5 22.7 %all_gather.7 = f32[8,2048]{1,0:T(8,128)S(1)} all-gather(f32[8,128]{1,0:T(8,128)S(1)} %convert_element_type.28), channel_id=1, replica_groups=mesh['gx'=16,'gy'=16] {'gy'}, dimensions={1}, use_global_device_ids=true | all-gather | bytes 69632 | tf_op jit(solution)/shard_map/all_gather | solution.py:90
  58.3 4.4 %all-to-all-start = ((f32[16,48,128]{2,0,1:T(8,128)}), f32[16,48,128]{2,0,1:T(8,128)S(1)}, u32[]{:S(2)}, u32[]{:S(2)}) async-start(f32[16,48,128]{2,0,1:T(8,128)} %copy.48), calls=%async_computation | async-start | bytes 786432 | tf_op jit(solution)/shard_map/all_to_all | solution.py:73
  63.1 1.7 collective-permute-start
  64.8 4.1 %collective-permute-start.1 = (f32[7,1,2048]{2,1,0:T(1,128)S(1)}, f32[7,1,2048]{2,1,0:T(1,128)S(1)}, u32[]{:S(2)}, u32[]{:S(2)}) collective-permute-start(f32[7,1,2048]{2,1,0:T(1,128)S(1)} %get-tuple-element.6), channel_id=1, source_target_pairs={{16,0},{32,16},{48,32},{64,48},{80,64},{96,80},{112,96},{128,112},... | collective-permute-start | bytes 172040 | tf_op jit(solution)/shard_map/ppermute | solution.py:20
  69.0 3.6 %all-to-all-done = f32[16,48,128]{2,0,1:T(8,128)S(1)} async-done(((f32[16,48,128]{2,0,1:T(8,128)}), f32[16,48,128]{2,0,1:T(8,128)S(1)}, u32[]{:S(2)}, u32[]{:S(2)}) %all-to-all-start) | async-done | bytes 393248 | tf_op jit(solution)/shard_map/all_to_all | solution.py:73
  72.6 1.2 fusion.7
  74.4 56.3 %reduce-scatter.2.cloned.1.call-done = f32[16,3,128]{2,0,1:T(8,128)} async-done(((f32[256,3,128]{2,0,1:T(8,128)}), f32[16,3,128]{2,0,1:T(8,128)}) %reduce-scatter.2.cloned.1.call-update) | async-done | bytes 24592 | tf_op jit(solution)/shard_map/reduce_scatter | solution.py:78
  130.7 1.4 copy.50
  132.1 19.3 %all-to-all-start.1 = ((f32[16,3,128]{2,1,0:T(4,128)}), f32[16,3,128]{2,1,0:T(4,128)S(1)}, u32[]{:S(2)}, u32[]{:S(2)}) async-start(f32[16,3,128]{2,1,0:T(4,128)} %copy.50), calls=%async_computation.2 | async-start | bytes 65536 | tf_op jit(solution)/shard_map/all_to_all | solution.py:79
  151.3 7.3 %all-to-all-done.1 = f32[16,3,128]{2,1,0:T(4,128)S(1)} async-done(((f32[16,3,128]{2,1,0:T(4,128)}), f32[16,3,128]{2,1,0:T(4,128)S(1)}, u32[]{:S(2)}, u32[]{:S(2)}) %all-to-all-start.1) | async-done | bytes 24608 | tf_op jit(solution)/shard_map/all_to_all | solution.py:79
  159.9 3.7 %all-to-all-start.2 = ((f32[48,8,128]{2,1,0:T(8,128)}), f32[48,8,128]{2,1,0:T(8,128)S(1)}, u32[]{:S(2)}, u32[]{:S(2)}) async-start(f32[48,8,128]{2,1,0:T(8,128)} %multiply_multiply_fusion), calls=%async_computation.3 | async-start | bytes 393216 | tf_op jit(solution)/shard_map/all_to_all | solution.py:91
  163.7 8.1 %all-to-all-done.2 = f32[48,8,128]{2,1,0:T(8,128)S(1)} async-done(((f32[48,8,128]{2,1,0:T(8,128)}), f32[48,8,128]{2,1,0:T(8,128)S(1)}, u32[]{:S(2)}, u32[]{:S(2)}) %all-to-all-start.2) | async-done | bytes 196640 | tf_op jit(solution)/shard_map/all_to_all | solution.py:91
  174.6 2.6 %collective-permute-done.3 = f32[3,1,2048]{2,1,0:T(1,128)S(1)} collective-permute-done((f32[3,1,2048]{2,1,0:T(1,128)S(1)}, f32[3,1,2048]{2,1,0:T(1,128)S(1)}, u32[]{:S(2)}, u32[]{:S(2)}) %collective-permute-start.3) | collective-permute-done | bytes 24608 | tf_op jit(solution)/shard_map/ppermute | solution.py:17
  178.0 1.5 collective-permute-start.5
  179.4 1.2 collective-permute-done.4
  180.6 2.2 collective-permute-done.5
  183.6 1.5 collective-permute-start.7
  185.1 1.2 collective-permute-done.6
  186.3 2.4 %collective-permute-done.7 = f32[3,1,2048]{2,1,0:T(1,128)S(1)} collective-permute-done((f32[3,1,2048]{2,1,0:T(1,128)S(1)}, f32[3,1,2048]{2,1,0:T(1,128)S(1)}, u32[]{:S(2)}, u32[]{:S(2)}) %collective-permute-start.7) | collective-permute-done | bytes 24608 | tf_op jit(solution)/shard_map/ppermute | solution.py:17
  189.5 1.5 collective-permute-start.9
  190.9 1.5 collective-permute-done.8
  192.4 1.9 collective-permute-done.9
  195.0 3.0 %copy.55 = f32[3,8,2048]{1,0,2:T(4,128)} copy(f32[3,8,2048]{2,1,0:T(8,128)S(1)} %fusion.13) | data formatting | bytes 393216 | tf_op jit(solution)/shard_map/add | solution.py:30
  198.0 4.4 %reshape.39 = f32[16,1,3072]{2,1,0:T(1,128)S(1)} reshape(f32[2048,3,8]{2,1,0:T(4,128)} %bitcast.57) | data formatting | bytes 393216
  202.5 16.5 %all_to_all.75 = f32[16,1,3072]{2,1,0:T(1,128)S(1)} all-to-all(f32[16,1,3072]{2,1,0:T(1,128)S(1)} %reshape.39), channel_id=1, replica_groups=mesh['gx'=16,'gy'=16] {'gy'}, dimensions={0} | all-to-all | bytes 393216 | tf_op jit(solution)/shard_map/all_to_all | solution.py:101
  220.6 4.1 %reshape.40 = f32[2048,3,8]{2,1,0:T(4,128)} reshape(f32[16,3072]{1,0:T(8,128)S(1)} %reduce) | data formatting | bytes 393216
  224.7 3.3 %copy.56 = f32[3,8,16,128]{3,1,0,2:T(8,128)S(1)} copy(f32[3,8,16,128]{1,0,3,2:T(4,128)} %bitcast.58) | data formatting | bytes 393216 | tf_op jit(solution)/shard_map/all_to_all | solution.py:101
  (57 shorter events, 14.0 us)
Async XLA Ops:
  6.5 152.1 %copy-start = (f32[48,48]{1,0:T(8,128)S(1)}, f32[48,48]{1,0:T(8,128)}, u32[]{:S(2)}) copy-start(f32[48,48]{1,0:T(8,128)} %param.19) | copy-start | bytes 27652
  8.3 49.9 %all-to-all-start.3 = ((f32[2,48,8,128]{3,2,0,1:T(8,128)}), f32[2,48,8,128]{3,2,0,1:T(8,128)S(1)}, u32[]{:S(2)}, u32[]{:S(2)}) async-start(f32[2,48,8,128]{3,2,0,1:T(8,128)} %pad_maximum_fusion), calls=%async_computation.4 | async-start | bytes 786432 | tf_op jit(solution)/shard_map/all_to_all | solution.py:87
  58.3 14.3 %all-to-all-start = ((f32[16,48,128]{2,0,1:T(8,128)}), f32[16,48,128]{2,0,1:T(8,128)S(1)}, u32[]{:S(2)}, u32[]{:S(2)}) async-start(f32[16,48,128]{2,0,1:T(8,128)} %copy.48), calls=%async_computation | async-start | bytes 786432 | tf_op jit(solution)/shard_map/all_to_all | solution.py:73
  62.7 68.0 %reduce-scatter.2.cloned.1.call-start = ((), (), s32[]{:S(2)}) async-start(), calls=%async_computation.6 | async-start | bytes 417792 | tf_op jit(solution)/shard_map/reduce_scatter | solution.py:78
  62.9 96.3 %copy-start.1 = (f32[48,8,128]{2,1,0:T(8,128)S(1)}, f32[48,8,128]{2,1,0:T(8,128)}, u32[]{:S(2)}) copy-start(f32[48,8,128]{2,1,0:T(8,128)} %param.17) | copy-start | bytes 589828
  63.1 10.7 %collective-permute-start = (f32[7,1,2048]{2,1,0:T(1,128)S(1)}, f32[7,1,2048]{2,1,0:T(1,128)S(1)}, u32[]{:S(2)}, u32[]{:S(2)}) collective-permute-start(f32[7,1,2048]{2,1,0:T(1,128)S(1)} %get-tuple-element.5), channel_id=1, source_target_pairs={{0,16},{16,32},{32,48},{48,64},{64,80},{80,96},{96,112},{112,128},... | collective-permute-start | bytes 172040 | tf_op jit(solution)/shard_map/ppermute | solution.py:17
  64.8 9.0 %collective-permute-start.1 = (f32[7,1,2048]{2,1,0:T(1,128)S(1)}, f32[7,1,2048]{2,1,0:T(1,128)S(1)}, u32[]{:S(2)}, u32[]{:S(2)}) collective-permute-start(f32[7,1,2048]{2,1,0:T(1,128)S(1)} %get-tuple-element.6), channel_id=1, source_target_pairs={{16,0},{32,16},{48,32},{64,48},{80,64},{96,80},{112,96},{128,112},... | collective-permute-start | bytes 172040 | tf_op jit(solution)/shard_map/ppermute | solution.py:20
  132.1 26.6 %all-to-all-start.1 = ((f32[16,3,128]{2,1,0:T(4,128)}), f32[16,3,128]{2,1,0:T(4,128)S(1)}, u32[]{:S(2)}, u32[]{:S(2)}) async-start(f32[16,3,128]{2,1,0:T(4,128)} %copy.50), calls=%async_computation.2 | async-start | bytes 65536 | tf_op jit(solution)/shard_map/all_to_all | solution.py:79
  159.9 11.9 %all-to-all-start.2 = ((f32[48,8,128]{2,1,0:T(8,128)}), f32[48,8,128]{2,1,0:T(8,128)S(1)}, u32[]{:S(2)}, u32[]{:S(2)}) async-start(f32[48,8,128]{2,1,0:T(8,128)} %multiply_multiply_fusion), calls=%async_computation.3 | async-start | bytes 393216 | tf_op jit(solution)/shard_map/all_to_all | solution.py:91
  171.9 2.8 %collective-permute-start.2 = (f32[3,1,2048]{2,1,0:T(1,128)S(1)}, f32[3,1,2048]{2,1,0:T(1,128)S(1)}, u32[]{:S(2)}, u32[]{:S(2)}) collective-permute-start(f32[3,1,2048]{2,1,0:T(1,128)S(1)} %get-tuple-element.16), channel_id=1, source_target_pairs={{16,0},{32,16},{48,32},{64,48},{80,64},{96,80},{112,96},{128,112},... | collective-permute-start | bytes 73736 | tf_op jit(solution)/shard_map/ppermute | solution.py:20
  172.4 4.8 %collective-permute-start.3 = (f32[3,1,2048]{2,1,0:T(1,128)S(1)}, f32[3,1,2048]{2,1,0:T(1,128)S(1)}, u32[]{:S(2)}, u32[]{:S(2)}) collective-permute-start(f32[3,1,2048]{2,1,0:T(1,128)S(1)} %get-tuple-element.15), channel_id=1, source_target_pairs={{0,16},{16,32},{32,48},{48,64},{64,80},{80,96},{96,112},{112,128},... | collective-permute-start | bytes 73736 | tf_op jit(solution)/shard_map/ppermute | solution.py:17
  177.9 2.8 %collective-permute-start.4 = (f32[3,1,2048]{2,1,0:T(1,128)S(1)}, f32[3,1,2048]{2,1,0:T(1,128)S(1)}, u32[]{:S(2)}, u32[]{:S(2)}) collective-permute-start(f32[3,1,2048]{2,1,0:T(1,128)S(1)} %get-tuple-element.14), channel_id=1, source_target_pairs={{16,0},{32,16},{48,32},{64,48},{80,64},{96,80},{112,96},{128,112},... | collective-permute-start | bytes 73736 | tf_op jit(solution)/shard_map/ppermute | solution.py:20
  178.0 4.9 %collective-permute-start.5 = (f32[3,1,2048]{2,1,0:T(1,128)S(1)}, f32[3,1,2048]{2,1,0:T(1,128)S(1)}, u32[]{:S(2)}, u32[]{:S(2)}) collective-permute-start(f32[3,1,2048]{2,1,0:T(1,128)S(1)} %get-tuple-element.13), channel_id=1, source_target_pairs={{0,16},{16,32},{32,48},{48,64},{64,80},{80,96},{96,112},{112,128},... | collective-permute-start | bytes 73736 | tf_op jit(solution)/shard_map/ppermute | solution.py:17
  183.5 2.8 %collective-permute-start.6 = (f32[3,1,2048]{2,1,0:T(1,128)S(1)}, f32[3,1,2048]{2,1,0:T(1,128)S(1)}, u32[]{:S(2)}, u32[]{:S(2)}) collective-permute-start(f32[3,1,2048]{2,1,0:T(1,128)S(1)} %get-tuple-element.12), channel_id=1, source_target_pairs={{16,0},{32,16},{48,32},{64,48},{80,64},{96,80},{112,96},{128,112},... | collective-permute-start | bytes 73736 | tf_op jit(solution)/shard_map/ppermute | solution.py:20
  183.6 5.0 %collective-permute-start.7 = (f32[3,1,2048]{2,1,0:T(1,128)S(1)}, f32[3,1,2048]{2,1,0:T(1,128)S(1)}, u32[]{:S(2)}, u32[]{:S(2)}) collective-permute-start(f32[3,1,2048]{2,1,0:T(1,128)S(1)} %get-tuple-element.11), channel_id=1, source_target_pairs={{0,16},{16,32},{32,48},{48,64},{64,80},{80,96},{96,112},{112,128},... | collective-permute-start | bytes 73736 | tf_op jit(solution)/shard_map/ppermute | solution.py:17
  189.4 3.0 %collective-permute-start.8 = (f32[3,1,2048]{2,1,0:T(1,128)S(1)}, f32[3,1,2048]{2,1,0:T(1,128)S(1)}, u32[]{:S(2)}, u32[]{:S(2)}) collective-permute-start(f32[3,1,2048]{2,1,0:T(1,128)S(1)} %get-tuple-element.10), channel_id=1, source_target_pairs={{16,0},{32,16},{48,32},{64,48},{80,64},{96,80},{112,96},{128,112},... | collective-permute-start | bytes 73736 | tf_op jit(solution)/shard_map/ppermute | solution.py:20
  189.5 4.9 %collective-permute-start.9 = (f32[3,1,2048]{2,1,0:T(1,128)S(1)}, f32[3,1,2048]{2,1,0:T(1,128)S(1)}, u32[]{:S(2)}, u32[]{:S(2)}) collective-permute-start(f32[3,1,2048]{2,1,0:T(1,128)S(1)} %get-tuple-element.9), channel_id=1, source_target_pairs={{0,16},{16,32},{32,48},{48,64},{64,80},{80,96},{96,112},{112,128},... | collective-permute-start | bytes 73736 | tf_op jit(solution)/shard_map/ppermute | solution.py:17
Sparse Core Ops, SparseCore 0:
  73.9 56.7 reduce-scatter.1
where the time goes:
time: 237 us; the launch traced here: 236 us
  waiting for transfers between devices  89.4 us (38%)
  blocking collectives  50.5 us (21%)
  starting transfers between devices  47.9 us (20%)
  local copies, waits for them, and re-layouts  20.5 us (9%)
  between operations  15 us (6%)
  other arithmetic  9.19 us (4%)
  matrix products  3.35 us (1%)
    reduce_scatter x1, waiting for transfers between devices, local(): mine = lax.psum_scatter(partial, 'gx', scatter_dimension=0, tiled=True)  56.3 us
    all_gather x1, blocking collectives, local(): mask_whole = lax.all_gather(mask, 'gy', axis=1, tiled=True)  22.7 us
    all_to_all x1, starting transfers between devices, local(): lax.all_to_all(mine, 'gy', split_axis=0, concat_axis=1, tiled=True)[0]  19.3 us
    all_to_all x1, blocking collectives, local(): field = lax.all_to_all(field, 'gy', split_axis=2, concat_axis=0, tiled=True)  16.5 us
    unnamed x1, blocking collectives  11.3 us
    unnamed x10, local copies, waits for them, and re-layouts  10.7 us
    ppermute x5, waiting for transfers between devices, extended(): lax.ppermute(lax.slice_in_dim(block, block.shape[dim] - width, None, axis...  9.05 us
    all_to_all x1, starting transfers between devices, local(): lax.all_to_all(jnp.stack([diff_x, diff_y]), 'gy', split_axis=1, concat_ax...  8.45 us
  transfers between devices with their start and end apart: 15, of which 12 were waited for; matrix products, arithmetic and copies ran while one was open for 4% of the time, Pallas kernels for 0%

commit v1 on v0

--- a/solution.py
+++ b/solution.py
@@ -87,7 +87,9 @@
     moved = lax.all_to_all(
         jnp.stack([diff_x, diff_y]), "gy", split_axis=1, concat_axis=3, tiled=True
     )
-    mask_whole = lax.all_gather(mask, "gy", axis=1, tiled=True)
+    mask_whole = jnp.concatenate(
+        lax.all_to_all(jnp.stack([mask] * lax.axis_size("gy")), "gy", 0, 0), axis=1
+    )
     field = lax.all_to_all(forcing, "gy", split_axis=0, concat_axis=2, tiled=True)
     group = field.shape[0]
     stacked = jnp.concatenate([moved[0], moved[1], mask_whole[None]], axis=0)

time: 237 us -> 229 us (0.966)
  blocking collectives: 50.5 us -> 27.9 us
  waiting for transfers between devices: 89.4 us -> 97.6 us
  starting transfers between devices: 47.9 us -> 53.8 us
    all_gather x1 -> x0, blocking collectives: 22.7 us -> none  [local(): mask_whole = lax.all_gather(mask, 'gy', axis=1, tiled=True)]
    all_to_all x1, waiting for transfers between devices: 0.01 us -> 7.66 us  [local(): lax.all_to_all(jnp.stack([diff_x, diff_y]), 'gy', split_axis=1, concat_ax...]
    all_to_all x0 -> x1, starting transfers between devices: none -> 4.33 us  [local(): lax.all_to_all(jnp.stack([mask] * lax.axis_size('gy')), 'gy', 0, 0)]
  transfers between devices with their start and end apart: 15 -> 16, of which waited for: 12 -> 13; matrix products, arithmetic and copies ran while one was open for 4% -> 4% of each run, Pallas kernels for 0% -> 0%
where the time goes in v1:
time: 229 us; the launch traced here: 228 us
  waiting for transfers between devices  97.6 us (43%)
  starting transfers between devices  53.8 us (23%)
  blocking collectives  27.9 us (12%)
  local copies, waits for them, and re-layouts  21.1 us (9%)
  between operations  14.9 us (7%)
  other arithmetic  9.2 us (4%)
  matrix products  3.35 us (1%)
    reduce_scatter x1, waiting for transfers between devices, local(): mine = lax.psum_scatter(partial, 'gx', scatter_dimension=0, tiled=True)  56.4 us
    all_to_all x1, starting transfers between devices, local(): lax.all_to_all(mine, 'gy', split_axis=0, concat_axis=1, tiled=True)[0]  19 us
    all_to_all x1, blocking collectives, local(): field = lax.all_to_all(field, 'gy', split_axis=2, concat_axis=0, tiled=True)  16.5 us
    unnamed x1, blocking collectives  11.4 us
    unnamed x10, local copies, waits for them, and re-layouts  10.6 us
    ppermute x5, waiting for transfers between devices, extended(): lax.ppermute(lax.slice_in_dim(block, block.shape[dim] - width, None, axis...  9.09 us
    all_to_all x1, starting transfers between devices, local(): lax.all_to_all(jnp.stack([diff_x, diff_y]), 'gy', split_axis=1, concat_ax...  8.45 us
    all_to_all x1, waiting for transfers between devices, local(): lax.all_to_all(forcing, 'gy', split_axis=0, concat_axis=2, tiled=True)  8.12 us
  transfers between devices with their start and end apart: 16, of which 13 were waited for; matrix products, arithmetic and copies ran while one was open for 4% of the time, Pallas kernels for 0%

profile of v1, /device:TPU:1, one launch (start us, length us, event | category | flops | bytes accessed | tf_op | source)
XLA Modules:
  0.0 227.9 jit_solution(3294439130420318315)
XLA Ops:
  6.5 1.8 pad_maximum_fusion
  8.3 8.4 %all-to-all-start.3 = ((f32[2,48,8,128]{3,2,0,1:T(8,128)}), f32[2,48,8,128]{3,2,0,1:T(8,128)S(1)}, u32[]{:S(2)}, u32[]{:S(2)}) async-start(f32[2,48,8,128]{3,2,0,1:T(8,128)} %pad_maximum_fusion), calls=%async_computation.4 | async-start | bytes 786432 | tf_op jit(solution)/shard_map/all_to_all | solution.py:87
  18.9 7.7 %all-to-all-done.3 = f32[2,48,8,128]{3,2,0,1:T(8,128)S(1)} async-done(((f32[2,48,8,128]{3,2,0,1:T(8,128)}), f32[2,48,8,128]{3,2,0,1:T(8,128)S(1)}, u32[]{:S(2)}, u32[]{:S(2)}) %all-to-all-start.3) | async-done | bytes 393248 | tf_op jit(solution)/shard_map/all_to_all | solution.py:87
  27.2 4.3 %all-to-all-start.4 = ((f32[16,8,128]{2,1,0:T(8,128)}), f32[16,8,128]{2,1,0:T(8,128)S(1)}, u32[]{:S(2)}, u32[]{:S(2)}) async-start(f32[16,8,128]{2,1,0:T(8,128)} %stack.11), calls=%async_computation.5 | async-start | bytes 131072 | tf_op jit(solution)/shard_map/all_to_all | solution.py:91
  31.5 1.7 fusion
  34.1 1.2 dynamic-slice
  36.7 11.4 %all-reduce.5 = s32[256]{0:T(256)S(1)} all-reduce(s32[256]{0:T(256)S(1)} %dynamic-update-slice), channel_id=1, replica_groups=mesh['gx'=16,'gy'=16] {'gy'}, use_global_device_ids=true, to_apply=%add.5 | all-reduce | flops 256 | bytes 2048
  48.3 6.3 %all-to-all-start = ((f32[16,48,128]{2,0,1:T(8,128)}), f32[16,48,128]{2,0,1:T(8,128)S(1)}, u32[]{:S(2)}, u32[]{:S(2)}) async-start(f32[16,48,128]{2,0,1:T(8,128)} %copy.48), calls=%async_computation | async-start | bytes 786432 | tf_op jit(solution)/shard_map/all_to_all | solution.py:73
  54.8 1.7 collective-permute-start
  56.6 4.1 %collective-permute-start.1 = (f32[7,1,2048]{2,1,0:T(1,128)S(1)}, f32[7,1,2048]{2,1,0:T(1,128)S(1)}, u32[]{:S(2)}, u32[]{:S(2)}) collective-permute-start(f32[7,1,2048]{2,1,0:T(1,128)S(1)} %get-tuple-element.6), channel_id=1, source_target_pairs={{16,0},{32,16},{48,32},{64,48},{80,64},{96,80},{112,96},{128,112},... | collective-permute-start | bytes 172040 | tf_op jit(solution)/shard_map/ppermute | solution.py:20
  60.7 3.9 %all-to-all-done = f32[16,48,128]{2,0,1:T(8,128)S(1)} async-done(((f32[16,48,128]{2,0,1:T(8,128)}), f32[16,48,128]{2,0,1:T(8,128)S(1)}, u32[]{:S(2)}, u32[]{:S(2)}) %all-to-all-start) | async-done | bytes 393248 | tf_op jit(solution)/shard_map/all_to_all | solution.py:73
  66.5 56.4 %reduce-scatter.2.cloned.1.call-done = f32[16,3,128]{2,0,1:T(8,128)} async-done(((f32[256,3,128]{2,0,1:T(8,128)}), f32[16,3,128]{2,0,1:T(8,128)}) %reduce-scatter.2.cloned.1.call-update) | async-done | bytes 24592 | tf_op jit(solution)/shard_map/reduce_scatter | solution.py:78
  123.0 1.4 copy.50
  124.3 19.0 %all-to-all-start.1 = ((f32[16,3,128]{2,1,0:T(4,128)}), f32[16,3,128]{2,1,0:T(4,128)S(1)}, u32[]{:S(2)}, u32[]{:S(2)}) async-start(f32[16,3,128]{2,1,0:T(4,128)} %copy.50), calls=%async_computation.2 | async-start | bytes 65536 | tf_op jit(solution)/shard_map/all_to_all | solution.py:79
  143.3 7.3 %all-to-all-done.1 = f32[16,3,128]{2,1,0:T(4,128)S(1)} async-done(((f32[16,3,128]{2,1,0:T(4,128)}), f32[16,3,128]{2,1,0:T(4,128)S(1)}, u32[]{:S(2)}, u32[]{:S(2)}) %all-to-all-start.1) | async-done | bytes 24608 | tf_op jit(solution)/shard_map/all_to_all | solution.py:79
  151.8 3.7 %all-to-all-start.2 = ((f32[48,8,128]{2,1,0:T(8,128)}), f32[48,8,128]{2,1,0:T(8,128)S(1)}, u32[]{:S(2)}, u32[]{:S(2)}) async-start(f32[48,8,128]{2,1,0:T(8,128)} %multiply_multiply_fusion), calls=%async_computation.3 | async-start | bytes 393216 | tf_op jit(solution)/shard_map/all_to_all | solution.py:93
  155.7 8.1 %all-to-all-done.2 = f32[48,8,128]{2,1,0:T(8,128)S(1)} async-done(((f32[48,8,128]{2,1,0:T(8,128)}), f32[48,8,128]{2,1,0:T(8,128)S(1)}, u32[]{:S(2)}, u32[]{:S(2)}) %all-to-all-start.2) | async-done | bytes 196640 | tf_op jit(solution)/shard_map/all_to_all | solution.py:93
  166.6 2.6 %collective-permute-done.3 = f32[3,1,2048]{2,1,0:T(1,128)S(1)} collective-permute-done((f32[3,1,2048]{2,1,0:T(1,128)S(1)}, f32[3,1,2048]{2,1,0:T(1,128)S(1)}, u32[]{:S(2)}, u32[]{:S(2)}) %collective-permute-start.3) | collective-permute-done | bytes 24608 | tf_op jit(solution)/shard_map/ppermute | solution.py:17
  170.0 1.5 collective-permute-start.5
  171.4 1.2 collective-permute-done.4
  172.7 2.2 collective-permute-done.5
  175.6 1.5 collective-permute-start.7
  177.1 1.2 collective-permute-done.6
  178.3 2.4 %collective-permute-done.7 = f32[3,1,2048]{2,1,0:T(1,128)S(1)} collective-permute-done((f32[3,1,2048]{2,1,0:T(1,128)S(1)}, f32[3,1,2048]{2,1,0:T(1,128)S(1)}, u32[]{:S(2)}, u32[]{:S(2)}) %collective-permute-start.7) | collective-permute-done | bytes 24608 | tf_op jit(solution)/shard_map/ppermute | solution.py:17
  181.5 1.5 collective-permute-start.9
  182.9 1.5 collective-permute-done.8
  184.4 1.9 collective-permute-done.9
  187.0 3.0 %copy.55 = f32[3,8,2048]{1,0,2:T(4,128)} copy(f32[3,8,2048]{2,1,0:T(8,128)S(1)} %fusion.13) | data formatting | bytes 393216 | tf_op jit(solution)/shard_map/add | solution.py:30
  190.0 4.4 %reshape.45 = f32[16,1,3072]{2,1,0:T(1,128)S(1)} reshape(f32[2048,3,8]{2,1,0:T(4,128)} %bitcast.59) | data formatting | bytes 393216
  194.5 16.5 %all_to_all.80 = f32[16,1,3072]{2,1,0:T(1,128)S(1)} all-to-all(f32[16,1,3072]{2,1,0:T(1,128)S(1)} %reshape.45), channel_id=1, replica_groups=mesh['gx'=16,'gy'=16] {'gy'}, dimensions={0} | all-to-all | bytes 393216 | tf_op jit(solution)/shard_map/all_to_all | solution.py:103
  212.6 4.0 %reshape.46 = f32[2048,3,8]{2,1,0:T(4,128)} reshape(f32[16,3072]{1,0:T(8,128)S(1)} %reduce) | data formatting | bytes 393216
  216.6 3.3 %copy.56 = f32[3,8,16,128]{3,1,0,2:T(8,128)S(1)} copy(f32[3,8,16,128]{1,0,3,2:T(4,128)} %bitcast.60) | data formatting | bytes 393216 | tf_op jit(solution)/shard_map/all_to_all | solution.py:103
  (59 shorter events, 15.8 us)
Async XLA Ops:
  6.5 144.1 %copy-start = (f32[48,48]{1,0:T(8,128)S(1)}, f32[48,48]{1,0:T(8,128)}, u32[]{:S(2)}) copy-start(f32[48,48]{1,0:T(8,128)} %param.19) | copy-start | bytes 27652
  8.3 18.2 %all-to-all-start.3 = ((f32[2,48,8,128]{3,2,0,1:T(8,128)}), f32[2,48,8,128]{3,2,0,1:T(8,128)S(1)}, u32[]{:S(2)}, u32[]{:S(2)}) async-start(f32[2,48,8,128]{3,2,0,1:T(8,128)} %pad_maximum_fusion), calls=%async_computation.4 | async-start | bytes 786432 | tf_op jit(solution)/shard_map/all_to_all | solution.py:87
  27.2 21.0 %all-to-all-start.4 = ((f32[16,8,128]{2,1,0:T(8,128)}), f32[16,8,128]{2,1,0:T(8,128)S(1)}, u32[]{:S(2)}, u32[]{:S(2)}) async-start(f32[16,8,128]{2,1,0:T(8,128)} %stack.11), calls=%async_computation.5 | async-start | bytes 131072 | tf_op jit(solution)/shard_map/all_to_all | solution.py:91
  48.3 16.3 %all-to-all-start = ((f32[16,48,128]{2,0,1:T(8,128)}), f32[16,48,128]{2,0,1:T(8,128)S(1)}, u32[]{:S(2)}, u32[]{:S(2)}) async-start(f32[16,48,128]{2,0,1:T(8,128)} %copy.48), calls=%async_computation | async-start | bytes 786432 | tf_op jit(solution)/shard_map/all_to_all | solution.py:73
  54.6 68.4 %reduce-scatter.2.cloned.1.call-start = ((), (), s32[]{:S(2)}) async-start(), calls=%async_computation.7 | async-start | bytes 417792 | tf_op jit(solution)/shard_map/reduce_scatter | solution.py:78
  54.7 96.5 %copy-start.1 = (f32[48,8,128]{2,1,0:T(8,128)S(1)}, f32[48,8,128]{2,1,0:T(8,128)}, u32[]{:S(2)}) copy-start(f32[48,8,128]{2,1,0:T(8,128)} %param.17) | copy-start | bytes 589828
  54.8 11.0 %collective-permute-start = (f32[7,1,2048]{2,1,0:T(1,128)S(1)}, f32[7,1,2048]{2,1,0:T(1,128)S(1)}, u32[]{:S(2)}, u32[]{:S(2)}) collective-permute-start(f32[7,1,2048]{2,1,0:T(1,128)S(1)} %get-tuple-element.5), channel_id=1, source_target_pairs={{0,16},{16,32},{32,48},{48,64},{64,80},{80,96},{96,112},{112,128},... | collective-permute-start | bytes 172040 | tf_op jit(solution)/shard_map/ppermute | solution.py:17
  56.6 9.3 %collective-permute-start.1 = (f32[7,1,2048]{2,1,0:T(1,128)S(1)}, f32[7,1,2048]{2,1,0:T(1,128)S(1)}, u32[]{:S(2)}, u32[]{:S(2)}) collective-permute-start(f32[7,1,2048]{2,1,0:T(1,128)S(1)} %get-tuple-element.6), channel_id=1, source_target_pairs={{16,0},{32,16},{48,32},{64,48},{80,64},{96,80},{112,96},{128,112},... | collective-permute-start | bytes 172040 | tf_op jit(solution)/shard_map/ppermute | solution.py:20
  124.3 26.3 %all-to-all-start.1 = ((f32[16,3,128]{2,1,0:T(4,128)}), f32[16,3,128]{2,1,0:T(4,128)S(1)}, u32[]{:S(2)}, u32[]{:S(2)}) async-start(f32[16,3,128]{2,1,0:T(4,128)} %copy.50), calls=%async_computation.2 | async-start | bytes 65536 | tf_op jit(solution)/shard_map/all_to_all | solution.py:79
  151.8 11.9 %all-to-all-start.2 = ((f32[48,8,128]{2,1,0:T(8,128)}), f32[48,8,128]{2,1,0:T(8,128)S(1)}, u32[]{:S(2)}, u32[]{:S(2)}) async-start(f32[48,8,128]{2,1,0:T(8,128)} %multiply_multiply_fusion), calls=%async_computation.3 | async-start | bytes 393216 | tf_op jit(solution)/shard_map/all_to_all | solution.py:93
  163.8 2.8 %collective-permute-start.2 = (f32[3,1,2048]{2,1,0:T(1,128)S(1)}, f32[3,1,2048]{2,1,0:T(1,128)S(1)}, u32[]{:S(2)}, u32[]{:S(2)}) collective-permute-start(f32[3,1,2048]{2,1,0:T(1,128)S(1)} %get-tuple-element.16), channel_id=1, source_target_pairs={{16,0},{32,16},{48,32},{64,48},{80,64},{96,80},{112,96},{128,112},... | collective-permute-start | bytes 73736 | tf_op jit(solution)/shard_map/ppermute | solution.py:20
  164.4 4.8 %collective-permute-start.3 = (f32[3,1,2048]{2,1,0:T(1,128)S(1)}, f32[3,1,2048]{2,1,0:T(1,128)S(1)}, u32[]{:S(2)}, u32[]{:S(2)}) collective-permute-start(f32[3,1,2048]{2,1,0:T(1,128)S(1)} %get-tuple-element.15), channel_id=1, source_target_pairs={{0,16},{16,32},{32,48},{48,64},{64,80},{80,96},{96,112},{112,128},... | collective-permute-start | bytes 73736 | tf_op jit(solution)/shard_map/ppermute | solution.py:17
  169.9 2.8 %collective-permute-start.4 = (f32[3,1,2048]{2,1,0:T(1,128)S(1)}, f32[3,1,2048]{2,1,0:T(1,128)S(1)}, u32[]{:S(2)}, u32[]{:S(2)}) collective-permute-start(f32[3,1,2048]{2,1,0:T(1,128)S(1)} %get-tuple-element.14), channel_id=1, source_target_pairs={{16,0},{32,16},{48,32},{64,48},{80,64},{96,80},{112,96},{128,112},... | collective-permute-start | bytes 73736 | tf_op jit(solution)/shard_map/ppermute | solution.py:20
  170.0 4.9 %collective-permute-start.5 = (f32[3,1,2048]{2,1,0:T(1,128)S(1)}, f32[3,1,2048]{2,1,0:T(1,128)S(1)}, u32[]{:S(2)}, u32[]{:S(2)}) collective-permute-start(f32[3,1,2048]{2,1,0:T(1,128)S(1)} %get-tuple-element.13), channel_id=1, source_target_pairs={{0,16},{16,32},{32,48},{48,64},{64,80},{80,96},{96,112},{112,128},... | collective-permute-start | bytes 73736 | tf_op jit(solution)/shard_map/ppermute | solution.py:17
  175.5 2.8 %collective-permute-start.6 = (f32[3,1,2048]{2,1,0:T(1,128)S(1)}, f32[3,1,2048]{2,1,0:T(1,128)S(1)}, u32[]{:S(2)}, u32[]{:S(2)}) collective-permute-start(f32[3,1,2048]{2,1,0:T(1,128)S(1)} %get-tuple-element.12), channel_id=1, source_target_pairs={{16,0},{32,16},{48,32},{64,48},{80,64},{96,80},{112,96},{128,112},... | collective-permute-start | bytes 73736 | tf_op jit(solution)/shard_map/ppermute | solution.py:20
  175.6 5.0 %collective-permute-start.7 = (f32[3,1,2048]{2,1,0:T(1,128)S(1)}, f32[3,1,2048]{2,1,0:T(1,128)S(1)}, u32[]{:S(2)}, u32[]{:S(2)}) collective-permute-start(f32[3,1,2048]{2,1,0:T(1,128)S(1)} %get-tuple-element.11), channel_id=1, source_target_pairs={{0,16},{16,32},{32,48},{48,64},{64,80},{80,96},{96,112},{112,128},... | collective-permute-start | bytes 73736 | tf_op jit(solution)/shard_map/ppermute | solution.py:17
  181.4 3.0 %collective-permute-start.8 = (f32[3,1,2048]{2,1,0:T(1,128)S(1)}, f32[3,1,2048]{2,1,0:T(1,128)S(1)}, u32[]{:S(2)}, u32[]{:S(2)}) collective-permute-start(f32[3,1,2048]{2,1,0:T(1,128)S(1)} %get-tuple-element.10), channel_id=1, source_target_pairs={{16,0},{32,16},{48,32},{64,48},{80,64},{96,80},{112,96},{128,112},... | collective-permute-start | bytes 73736 | tf_op jit(solution)/shard_map/ppermute | solution.py:20
  181.5 4.9 %collective-permute-start.9 = (f32[3,1,2048]{2,1,0:T(1,128)S(1)}, f32[3,1,2048]{2,1,0:T(1,128)S(1)}, u32[]{:S(2)}, u32[]{:S(2)}) collective-permute-start(f32[3,1,2048]{2,1,0:T(1,128)S(1)} %get-tuple-element.9), channel_id=1, source_target_pairs={{0,16},{16,32},{32,48},{48,64},{64,80},{80,96},{96,112},{112,128},... | collective-permute-start | bytes 73736 | tf_op jit(solution)/shard_map/ppermute | solution.py:17
Sparse Core Ops, SparseCore 0:
  66.0 56.9 reduce-scatter.1
